TPU v7x, 512 devices: a whole 4x4x16 slice. The times are simulated.
512 devices in a mesh: blk: 16 (over y, x_hi, core), group: 32 (over x_lo, z).
Axes of the slice: x: 4 (x_hi: 2, x_lo: 2; x = x_hi * 2 + x_lo), y: 4, z: 16, core: 2. Of those that a mesh axis runs over, the one named last changes fastest.
Arguments:
- student_features: bfloat16 [65536, 768], P(('blk', 'group')), may hold values from -8 to 8
- teacher_image: bfloat16 [65536, 1152], P(('blk', 'group')), may hold values from -8 to 8
- text_embeds: bfloat16 [65536, 1152], P(('blk', 'group')), may hold values from -8 to 8
- pair_ids: int32 [65536], replicated, may hold values from 0 to 8191
- head_weights: bfloat16 [1152, 768], replicated, may hold values from -1 to 1
- moment_first: float32 [1152, 768], P('group'), may hold values from -4 to 4
- moment_second: float32 [1152, 768], P('group'), may hold values from 0.01 to 0.3
Outputs:
- row_loss: float32 [65536], P(('blk', 'group'))
- new_first: float32 [1152, 768], P('group')
- new_second: float32 [1152, 768], P('group')
- new_weights: bfloat16 [1152, 768], replicated
All inputs are finite; a program needn't handle non-finite values.
Results may differ from a plain program's by a relative error of at most 0.0025.
The roundings to bfloat16 on the way count: a program that leaves them out, or rounds other values in their place, can miss the bound.
Values may be sent and summed in bfloat16 or wider, within the bound.
No kernel may reach another device: no remote copies, remote signals or barrier semaphores. Data moves between devices by JAX's collectives and lax.ppermute only.
A program may use at most 64 MiB of HBM per device.

v0:
```python
import jax
import jax.numpy as jnp
from jax import lax
from jax.sharding import PartitionSpec as P

student_scale = 20.0
student_bias = -1.0
teacher_scale = 25.0
teacher_bias = -1.5
label_mix = 0.5
norm_eps = 1e-06
beta_one = 0.9
beta_two = 0.95
learn_rate = 0.01
weight_decay = 0.0001
adam_eps = 1e-08
adam_step = 100.0


def from_partner(shard, axis, bit):
    return lax.ppermute(shard, axis, [(i, i ^ 1 << bit) for i in range(lax.axis_size(axis))])


def unit_rows(values):
    values = values.astype(jnp.float32)
    return values * lax.rsqrt(jnp.sum(values * values, axis=-1, keepdims=True) + norm_eps)


def pair_terms(student_rows, teacher_rows, left_ids, text_rows, right_ids):
    dims = (((1,), (1,)), ((), ()))
    student_logit = (
        student_scale
        * lax.dot_general(student_rows, text_rows, dims, preferred_element_type=jnp.float32)
        + student_bias
    )
    teacher_logit = (
        teacher_scale
        * lax.dot_general(teacher_rows, text_rows, dims, preferred_element_type=jnp.float32)
        + teacher_bias
    )
    labels = (left_ids[:, None] == right_ids[None, :]).astype(jnp.float32)
    target = (1.0 - label_mix) * labels + label_mix * jax.nn.sigmoid(teacher_logit)
    losses = jnp.sum(jax.nn.softplus(student_logit) - target * student_logit, axis=1)
    coeff = (jax.nn.sigmoid(student_logit) - target).astype(jnp.bfloat16)
    pulled = jnp.dot(coeff, text_rows, preferred_element_type=jnp.float32)
    return (losses, pulled)


def per_device(
    student_features,
    teacher_image,
    text_embeds,
    pair_ids,
    head_weights,
    moment_first,
    moment_second,
):
    row_count = student_features.shape[0]
    blk_count = lax.axis_size("blk")
    group_count = lax.axis_size("group")
    swap_bit = group_count.bit_length() - 2
    group_index = lax.axis_index("group")
    partner_index = (group_index + group_count // 2) % group_count
    blk_index = lax.axis_index("blk")
    projected = lax.dot_general(
        student_features, head_weights, (((1,), (1,)), ((), ())), preferred_element_type=jnp.float32
    )
    inverse = lax.rsqrt(jnp.sum(projected * projected, axis=-1, keepdims=True) + norm_eps)
    student = projected * inverse
    student_b = student.astype(jnp.bfloat16)
    teacher_b = unit_rows(teacher_image).astype(jnp.bfloat16)
    texts_b = unit_rows(text_embeds).astype(jnp.bfloat16)
    ids_grid = pair_ids.reshape(blk_count, group_count, row_count)
    own_ids = lax.dynamic_index_in_dim(ids_grid, group_index, 1, keepdims=False)
    far_ids = lax.dynamic_index_in_dim(ids_grid, partner_index, 1, keepdims=False)
    left_ids = lax.dynamic_index_in_dim(own_ids, blk_index, 0, keepdims=False)
    far_block = from_partner(texts_b, "group", swap_bit)
    paired = jnp.concatenate([texts_b, far_block], axis=0)
    paired_ids = jnp.stack([own_ids, far_ids], axis=1).reshape(-1)
    losses, pulled = pair_terms(
        student_b,
        teacher_b,
        left_ids,
        lax.all_gather(paired, "blk", axis=0, tiled=True),
        paired_ids,
    )
    totals = (losses, pulled)
    losses, pulled = totals
    row_loss = losses / row_count
    grad_student = student_scale / row_count * pulled
    grad_projected = (
        inverse * (grad_student - student * jnp.sum(student * grad_student, axis=-1, keepdims=True))
    ).astype(jnp.bfloat16)
    shard_rows = moment_first.shape[0]
    group_grad = lax.psum_scatter(
        lax.dot_general(
            grad_projected,
            student_features,
            (((0,), (0,)), ((), ())),
            preferred_element_type=jnp.float32,
        ),
        "group",
        scatter_dimension=0,
        tiled=True,
    )
    head_grad = lax.psum(group_grad, "blk")
    new_first = beta_one * moment_first + (1.0 - beta_one) * head_grad
    new_second = beta_two * moment_second + (1.0 - beta_two) * head_grad * head_grad
    first_hat = new_first / (1.0 - beta_one**adam_step)
    second_hat = new_second / (1.0 - beta_two**adam_step)
    own_weights = lax.dynamic_slice_in_dim(
        head_weights, group_index * shard_rows, shard_rows, 0
    ).astype(jnp.float32)
    updated = own_weights - learn_rate * (
        first_hat / (jnp.sqrt(second_hat) + adam_eps) + weight_decay * own_weights
    )
    new_weights = lax.all_gather(updated.astype(jnp.bfloat16), "group", axis=0, tiled=True)
    return (row_loss, new_first, new_second, new_weights)


def solution(mesh):
    placed = (
        P(("blk", "group"), None),
        P(("blk", "group"), None),
        P(("blk", "group"), None),
        P(),
        P(),
        P("group", None),
        P("group", None),
    )
    return jax.shard_map(
        per_device,
        mesh=mesh,
        in_specs=placed,
        out_specs=(P(("blk", "group")), P("group", None), P("group", None), P()),
        check_vma=False,
    )
```

profile of v0, /device:TPU:8, one launch (start us, length us, event | category | flops | bytes accessed | tf_op | source)
XLA Modules:
  0.0 531.9 jit_solution(12891333635255561007)
XLA Ops:
  7.2 1.3 fusion.12
  8.5 1.1 fusion.13
  9.6 3.4 collective-permute-start
  13.0 7.2 %collective-permute-done = bf16[128,1152]{1,0:T(8,128)(2,1)S(1)} collective-permute-done((bf16[128,1152]{1,0:T(8,128)(2,1)S(1)}, bf16[128,1152]{1,0:T(8,128)(2,1)S(1)}, u32[]{:S(2)}, u32[]{:S(2)}) %collective-permute-start) | collective-permute-done | bytes 294944 | tf_op jit(solution)/shard_map/ppermute | solution.py:21
  20.2 0.9 pad_maximum_fusion
  21.2 0.7 fusion.27
  21.9 0.9 constant_dynamic-slice_fusion.2
  23.0 0.8 multiply_reduce_fusion.1
  23.8 93.0 %all-gather.4.cloned.1.call-done = bf16[4096,1152]{1,0:T(8,128)(2,1)} async-done(((bf16[256,1152]{1,0:T(8,128)(2,1)}), bf16[4096,1152]{1,0:T(8,128)(2,1)}) %all-gather.4.cloned.1.call-update) | async-done | bytes 9437200 | tf_op jit(solution)/shard_map/all_gather | solution.py:84
  116.8 7.1 %fusion.8 = f32[128,4096]{1,0:T(8,128)S(1)} fusion(bf16[4096,1152]{1,0:T(8,128)(2,1)} %all-gather.4.cloned.1.call-done, s32[4096]{0:T(1024)S(1)} %bitcast.15, s32[128]{0:T(128)S(1)} %fusion.27, bf16[128,1152]{1,0:T(8,128)(2,1)S(1)} %copy-done.2, f32[128]{0:T(128)S(1)} %add_rsqrt_fusion), kind=kOutput, calls=%fused_computation.10 | convolution fusion | flops 1213120512 | bytes 11846656 | tf_op jit(solution)/shard_map/dot_general | solution.py:38
  123.8 3.8 fusion.10
  127.7 1.9 multiply_reduce_fusion
  129.5 2.5 fusion.16
  132.1 82.5 %fusion = f32[40,768]{1,0:T(8,128)S(1)} fusion(f32[1152,768]{1,0:T(8,128)} %fusion.16), kind=kCustom, calls=%all-reduce-scatter | all-reduce-scatter fusion | flops 983041 | bytes 3663872
  214.6 4.1 collective-permute-start.3
  218.7 1.5 collective-permute-start.2
  220.2 2.9 collective-permute-start.1
  223.1 5.6 %collective-permute-start.4 = (f32[4,768]{1,0:T(4,128)S(1)}, f32[4,768]{1,0:T(4,128)S(1)}, u32[]{:S(2)}, u32[]{:S(2)}) collective-permute-start(f32[4,768]{1,0:T(4,128)S(1)} %slice), channel_id=1, source_target_pairs={{0,4},{1,5},{2,6},{3,7},{4,8},{5,9},{6,10},{7,11},{8,12},{9,13},{1... | collective-permute-start | bytes 36872
  228.7 1.3 dynamic-slice.6
  231.3 0.7 constant_dynamic-slice_fusion
  232.1 149.7 %all-reduce.4.cloned.1.call-done = f32[36,768]{1,0:T(8,128)} async-done(((f32[36,768]{1,0:T(8,128)}), f32[36,768]{1,0:T(8,128)}) %all-reduce.4.cloned.1.call-update) | async-done | bytes 110608 | tf_op jit(solution)/shard_map/psum | solution.py:106
  381.7 1.7 fusion.26
  384.0 137.8 %all-gather.6.cloned.1.call-done = bf16[32,36,768]{2,1,0:T(8,128)(2,1)} async-done(((bf16[1,36,768]{2,1,0:T(8,128)(2,1)}), bf16[32,36,768]{2,1,0:T(8,128)(2,1)}) %all-gather.6.cloned.1.call-update) | async-done | bytes 1769488 | tf_op jit(solution)/shard_map/all_gather | solution.py:117
  521.8 3.6 reshape.37
  (30 shorter events, 1.5 us)
Async XLA Ops:
  7.2 15.8 %copy-start = (bf16[128,768]{1,0:T(8,128)(2,1)S(1)}, bf16[128,768]{1,0:T(8,128)(2,1)}, u32[]{:S(2)}) copy-start(bf16[128,768]{1,0:T(8,128)(2,1)} %param.7) | copy-start | bytes 589828
  7.2 15.6 %copy-start.2 = (bf16[128,1152]{1,0:T(8,128)(2,1)S(1)}, bf16[128,1152]{1,0:T(8,128)(2,1)}, u32[]{:S(2)}) copy-start(bf16[128,1152]{1,0:T(8,128)(2,1)} %param.8) | copy-start | bytes 884740
  7.2 15.8 %copy-start.1 = (bf16[1152,768]{1,0:T(8,128)(2,1)S(1)}, bf16[1152,768]{1,0:T(8,128)(2,1)}, u32[]{:S(2)}) copy-start(bf16[1152,768]{1,0:T(8,128)(2,1)} %param.11) | copy-start | bytes 5308420
  7.2 109.6 %all-gather.4.cloned.1.call-start = ((), (), s32[]{:S(2)}) async-start(), calls=%async_computation | async-start | bytes 10027008 | tf_op jit(solution)/shard_map/all_gather | solution.py:84
  9.6 10.6 %collective-permute-start = (bf16[128,1152]{1,0:T(8,128)(2,1)S(1)}, bf16[128,1152]{1,0:T(8,128)(2,1)S(1)}, u32[]{:S(2)}, u32[]{:S(2)}) collective-permute-start(bf16[128,1152]{1,0:T(8,128)(2,1)S(1)} %fusion.13), channel_id=1, source_target_pairs={{0,16},{1,17},{2,18},{3,19},{4,20},{5,21},{6,22},{7,23},{8,24},{9,... | collective-permute-start | bytes 884744 | tf_op jit(solution)/shard_map/ppermute | solution.py:21
  21.1 360.6 %all-reduce.4.cloned.1.call-start = ((), (), s32[]{:S(2)}) async-start(), calls=%async_computation.1 | async-start | bytes 245760 | tf_op jit(solution)/shard_map/psum | solution.py:106
  116.8 7.1 %copy-start.5 = (bf16[4096,1152]{1,0:T(8,128)(2,1)S(1)}, bf16[4096,1152]{1,0:T(8,128)(2,1)}, u32[]{:S(2)}) copy-start(bf16[4096,1152]{1,0:T(8,128)(2,1)} %all-gather.4.cloned.1.call-done) | copy-start | bytes 28311556
  132.1 249.7 %copy-start.3 = (f32[36,768]{1,0:T(8,128)S(1)}, f32[36,768]{1,0:T(8,128)}, u32[]{:S(2)}) copy-start(f32[36,768]{1,0:T(8,128)} %param.13) | copy-start | bytes 331780
  132.1 249.7 %copy-start.4 = (f32[36,768]{1,0:T(8,128)S(1)}, f32[36,768]{1,0:T(8,128)}, u32[]{:S(2)}) copy-start(f32[36,768]{1,0:T(8,128)} %param.12) | copy-start | bytes 331780
  214.6 16.1 %collective-permute-start.3 = (f32[40,768]{1,0:T(8,128)S(1)}, f32[40,768]{1,0:T(8,128)S(1)}, u32[]{:S(2)}, u32[]{:S(2)}) collective-permute-start(f32[40,768]{1,0:T(8,128)S(1)} %fusion), channel_id=1, source_target_pairs={{0,3},{1,4},{2,5},{3,6},{4,7},{5,8},{6,9},{7,10},{8,11},{9,12},{10... | collective-permute-start | bytes 368648
  218.7 12.0 %collective-permute-start.2 = (f32[40,768]{1,0:T(8,128)S(1)}, f32[40,768]{1,0:T(8,128)S(1)}, u32[]{:S(2)}, u32[]{:S(2)}) collective-permute-start(f32[40,768]{1,0:T(8,128)S(1)} %fusion), channel_id=1, source_target_pairs={{0,2},{1,3},{2,4},{3,5},{4,6},{5,7},{6,8},{7,9},{8,10},{9,11},{10,... | collective-permute-start | bytes 368648
  220.2 10.5 %collective-permute-start.1 = (f32[40,768]{1,0:T(8,128)S(1)}, f32[40,768]{1,0:T(8,128)S(1)}, u32[]{:S(2)}, u32[]{:S(2)}) collective-permute-start(f32[40,768]{1,0:T(8,128)S(1)} %fusion), channel_id=1, source_target_pairs={{0,1},{1,2},{2,3},{3,4},{4,5},{5,6},{6,7},{7,8},{8,9},{9,10},{10,1... | collective-permute-start | bytes 368648
  223.1 7.5 %collective-permute-start.4 = (f32[4,768]{1,0:T(4,128)S(1)}, f32[4,768]{1,0:T(4,128)S(1)}, u32[]{:S(2)}, u32[]{:S(2)}) collective-permute-start(f32[4,768]{1,0:T(4,128)S(1)} %slice), channel_id=1, source_target_pairs={{0,4},{1,5},{2,6},{3,7},{4,8},{5,9},{6,10},{7,11},{8,12},{9,13},{1... | collective-permute-start | bytes 36872
  232.0 289.8 %all-gather.6.cloned.1.call-start = ((), (), s32[]{:S(2)}) async-start(), calls=%async_computation.2 | async-start | bytes 2027520 | tf_op jit(solution)/shard_map/all_gather | solution.py:117
Sparse Core Ops, SparseCore 0:
  21.2 95.4 all-gather.3
  232.1 149.5 all-reduce.3
  384.4 137.3 all-gather.5
where the time goes:
time: 532 us
  waiting for transfers between devices  388 us (73%)
  blocking collectives  82.5 us (16%)
  starting transfers between devices  17.6 us (3%)
  matrix products  16.1 us (3%)
  between operations  14.6 us (3%)
  local copies, waits for them, and re-layouts  7.8 us (1%)
  other arithmetic  5.56 us (1%)
    psum x1, waiting for transfers between devices, per_device(): head_grad = lax.psum(group_grad, 'blk')  150 us
    all_gather x1, waiting for transfers between devices, per_device(): lax.all_gather(updated.astype(jnp.bfloat16), 'group', axis=0, tiled=True)  138 us
    all_gather x1, waiting for transfers between devices, per_device(): lax.all_gather(paired, 'blk', axis=0, tiled=True)  93 us
    unnamed x1, blocking collectives  82.5 us
    unnamed x4, starting transfers between devices  14.1 us
  transfers between devices with their start and end apart: 8, of which 4 were waited for; matrix products, arithmetic and copies ran while one was open for 1% of the time, Pallas kernels for 0%

commit v1 on v0

v1 whole, which is shorter than its diff:
```python
import jax
import jax.numpy as jnp
from jax import lax
from jax.sharding import PartitionSpec as P

student_scale = 20.0
student_bias = -1.0
teacher_scale = 25.0
teacher_bias = -1.5
label_mix = 0.5
norm_eps = 1e-06
beta_one = 0.9
beta_two = 0.95
learn_rate = 0.01
weight_decay = 0.0001
adam_eps = 1e-08
adam_step = 100.0

AXES = ("blk", "group")


def device(X, y, core, z):
    return (y * 4 + X % 2 * 2 + core) * 32 + X // 2 * 16 + z


def x_line(y, core, z):
    return [device(X, y, core, z) for X in range(4)]


def y_line(X, core, z):
    return [device(X, y, core, z) for y in range(4)]


def lines(along_x):
    groups = []
    for core in range(2):
        line = x_line if (core == 0) == along_x else y_line
        groups += [line(i, core, z) for z in range(16) for i in range(4)]
    return groups


FIRST = lines(True)
SECOND = lines(False)
PLANE = [
    [device(X, y, core, z) for X in range(4) for y in range(4)]
    for core in range(2)
    for z in range(16)
]
COLUMN = [
    [device(X, y, core, z) for z in range(16)]
    for X in range(4)
    for y in range(4)
    for core in range(2)
]
TWIN = [(i, i ^ 32) for i in range(512)]


def exchange(pieces, groups):
    return lax.all_to_all(pieces, AXES, 0, 0, axis_index_groups=groups, tiled=True)


def share(block, groups):
    return exchange(jnp.broadcast_to(block[None], (len(groups[0]), *block.shape)), groups)


def from_twin(shard):
    return lax.ppermute(shard, AXES, TWIN)


def unit_rows(values):
    values = values.astype(jnp.float32)
    return values * lax.rsqrt(jnp.sum(values * values, axis=-1, keepdims=True) + norm_eps)


def pair_terms(student_rows, teacher_rows, left_ids, text_rows, right_ids):
    dims = (((1,), (1,)), ((), ()))
    student_logit = (
        student_scale
        * lax.dot_general(student_rows, text_rows, dims, preferred_element_type=jnp.float32)
        + student_bias
    )
    teacher_logit = (
        teacher_scale
        * lax.dot_general(teacher_rows, text_rows, dims, preferred_element_type=jnp.float32)
        + teacher_bias
    )
    labels = (left_ids[:, None] == right_ids[None, :]).astype(jnp.float32)
    target = (1.0 - label_mix) * labels + label_mix * jax.nn.sigmoid(teacher_logit)
    losses = jnp.sum(jax.nn.softplus(student_logit) - target * student_logit, axis=1)
    coeff = (jax.nn.sigmoid(student_logit) - target).astype(jnp.bfloat16)
    pulled = jnp.dot(coeff, text_rows, preferred_element_type=jnp.float32)
    return (losses, pulled)


def row_order(core):
    place = lax.iota(jnp.int32, 1152)
    first, second = place // 288, place // 72 % 4
    X = jnp.where(core == 0, first, second)
    y = jnp.where(core == 0, second, first)
    return X * 288 + place // 9 % 8 * 36 + y * 9 + place % 9


def one_hot(index):
    return (index[:, None] == lax.iota(jnp.int32, 1152)[None, :]).astype(jnp.bfloat16)


def rounded(values):
    return lax.reduce_precision(values, 8, 7)


def per_device(
    student_features,
    teacher_image,
    text_embeds,
    pair_ids,
    head_weights,
    moment_first,
    moment_second,
):
    rows = student_features.shape[0]
    blk_index = lax.axis_index("blk")
    group_index = lax.axis_index("group")
    y, xh, core = blk_index // 4, blk_index // 2 % 2, blk_index % 2
    xl, z = group_index // 16, group_index % 16

    texts_b = unit_rows(text_embeds).astype(jnp.bfloat16)
    near = share(jnp.concatenate([texts_b, student_features], axis=1), FIRST)
    features = near[:, :, 1152:]
    texts = share(near[:, :, :1152].reshape(512, 1152), SECOND).reshape(2048, 1152)

    both_features = jnp.concatenate([student_features, from_twin(student_features)], axis=0)
    both_teacher = jnp.concatenate([teacher_image, from_twin(teacher_image)], axis=0)
    projected = lax.dot_general(
        both_features, head_weights, (((1,), (1,)), ((), ())), preferred_element_type=jnp.float32
    )
    inverse = lax.rsqrt(jnp.sum(projected * projected, axis=-1, keepdims=True) + norm_eps)
    student = projected * inverse
    student_b = student.astype(jnp.bfloat16)
    teacher_b = unit_rows(both_teacher).astype(jnp.bfloat16)

    ids_grid = pair_ids.reshape(4, 2, 2, 2, 16, rows)
    ids_plane = lax.dynamic_index_in_dim(ids_grid, z, 4, keepdims=False)
    ids_core = lax.dynamic_index_in_dim(ids_plane, core, 2, keepdims=False)
    ids_yx = ids_core.transpose(0, 2, 1, 3).reshape(4, 4, rows)
    text_ids = jnp.where(core == 0, ids_yx, ids_yx.transpose(1, 0, 2)).reshape(-1)
    ids_rows = pair_ids.reshape(512, rows)
    left_ids = jnp.concatenate(
        [
            lax.dynamic_index_in_dim(ids_rows, blk_index * 32 + group_index, 0, keepdims=False),
            lax.dynamic_index_in_dim(ids_rows, (blk_index ^ 1) * 32 + group_index, 0, keepdims=False),
        ]
    )
    losses, pulled = pair_terms(student_b, teacher_b, left_ids, texts, text_ids)

    pulled = pulled[:rows] + from_twin(pulled[rows:])
    student, inverse = student[:rows], inverse[:rows]
    grad_student = student_scale / rows * pulled
    grad_projected = (
        inverse * (grad_student - student * jnp.sum(student * grad_student, axis=-1, keepdims=True))
    ).astype(jnp.bfloat16)

    grad_rows = lax.dot_general(
        one_hot(row_order(core)),
        grad_projected,
        (((1,), (1,)), ((), ())),
        preferred_element_type=jnp.float32,
    ).astype(jnp.bfloat16)
    grad_rows = exchange(grad_rows.reshape(4, 288, rows), FIRST)
    line_grad = lax.dot_general(
        grad_rows, features, (((0, 2), (0, 1)), ((), ())), preferred_element_type=jnp.float32
    )
    core_grad = jnp.sum(exchange(line_grad.reshape(4, 72, 768), SECOND), axis=0)
    left, right = core_grad[:, :384], core_grad[:, 384:]
    other_losses = jnp.pad(losses[rows:].reshape(1, rows), ((0, 7), (0, 256)))
    arrived = from_twin(jnp.concatenate([jnp.where(core == 0, right, left), other_losses], axis=0))
    chip_grad = jnp.where(core == 0, left, right) + arrived[:72]
    row_loss = (losses[:rows] + arrived[72, :rows]) / rows

    plane_grad = chip_grad.reshape(8, 9, 384)
    own_grad = jnp.sum(exchange(jnp.concatenate([plane_grad, plane_grad], axis=0), COLUMN), axis=0)

    def adam(head_grad, first, second, weights):
        new_first = beta_one * first + (1.0 - beta_one) * head_grad
        new_second = beta_two * second + (1.0 - beta_two) * head_grad * head_grad
        first_hat = new_first / (1.0 - beta_one**adam_step)
        second_hat = new_second / (1.0 - beta_two**adam_step)
        weights = weights.astype(jnp.float32)
        updated = weights - learn_rate * (
            first_hat / (jnp.sqrt(second_hat) + adam_eps) + weight_decay * weights
        )
        return new_first, new_second, updated.astype(jnp.bfloat16)

    def piece(values, start):
        return lax.dynamic_slice(values, (start + y * 9, core * 384), (9, 384))

    _, _, own_weights = adam(
        own_grad,
        piece(moment_first, 0),
        piece(moment_second, 0),
        piece(head_weights, group_index * 36),
    )
    column = share(own_weights, COLUMN)
    chip_weights = lax.dynamic_slice_in_dim(column, xh * 8, 8, 0).reshape(72, 384)
    high = rounded(own_grad)
    middle = rounded(own_grad - high)
    low = own_grad - high - middle
    grad_parts = jnp.concatenate([high, middle, low], axis=0).astype(jnp.bfloat16)
    half = share(jnp.concatenate([chip_weights, grad_parts], axis=0), PLANE)
    twin_half = from_twin(half)
    whole = jnp.concatenate(
        [jnp.where(core == 0, half, twin_half), jnp.where(core == 0, twin_half, half)], axis=2
    )
    new_weights = lax.dot_general(
        one_hot(row_order(0)),
        whole[:, :72].reshape(1152, 768),
        (((0,), (0,)), ((), ())),
        preferred_element_type=jnp.float32,
    ).astype(jnp.bfloat16)
    parts = lax.dynamic_slice_in_dim(whole, (xl * 2 + z // 8) * 4, 4, 0)[:, 72:]
    parts = parts.reshape(4, 3, 9, 768).astype(jnp.float32)
    head_grad = ((parts[:, 0] + parts[:, 1]) + parts[:, 2]).reshape(36, 768)
    new_first = beta_one * moment_first + (1.0 - beta_one) * head_grad
    new_second = beta_two * moment_second + (1.0 - beta_two) * head_grad * head_grad
    return (row_loss, new_first, new_second, new_weights)


def solution(mesh):
    placed = (
        P(("blk", "group"), None),
        P(("blk", "group"), None),
        P(("blk", "group"), None),
        P(),
        P(),
        P("group", None),
        P("group", None),
    )
    return jax.shard_map(
        per_device,
        mesh=mesh,
        in_specs=placed,
        out_specs=(P(("blk", "group")), P("group", None), P("group", None), P()),
        check_vma=False,
    )
```

time: 532 us -> 207 us (0.39)
  the two profiles are of different devices: /device:TPU:8 before, /device:TPU:1 now
where the time goes in v1:
time: 207 us; the launch traced here: 204 us
  starting transfers between devices  62.5 us (30%)
  waiting for transfers between devices  58.2 us (28%)
  blocking collectives  44.7 us (22%)
  matrix products  22 us (11%)
  other arithmetic  8.46 us (4%)
  local copies, waits for them, and re-layouts  6.72 us (3%)
    all_to_all x4, waiting for transfers between devices, exchange(): lax.all_to_all(pieces, AXES, 0, 0, axis_index_groups=groups, tiled=True)  53.8 us
    all_to_all x3, blocking collectives, exchange(): lax.all_to_all(pieces, AXES, 0, 0, axis_index_groups=groups, tiled=True)  44.7 us
    all_to_all x4, starting transfers between devices, exchange(): lax.all_to_all(pieces, AXES, 0, 0, axis_index_groups=groups, tiled=True)  32.2 us
    ppermute x5, starting transfers between devices, from_twin(): return lax.ppermute(shard, AXES, TWIN)  30.2 us
    dot_general x1, matrix products, pair_terms(): lax.dot_general(student_rows, text_rows, dims, preferred_element_type=jnp...  4.91 us
    ppermute x5, waiting for transfers between devices, from_twin(): return lax.ppermute(shard, AXES, TWIN)  4.48 us
    dot_general x1, matrix products, pair_terms(): lax.dot_general(teacher_rows, text_rows, dims, preferred_element_type=jnp...  4.26 us
  transfers between devices with their start and end apart: 9, of which 7 were waited for; matrix products, arithmetic and copies ran while one was open for 3% of the time, Pallas kernels for 0%

profile of v1, /device:TPU:1, one launch (start us, length us, event | category | flops | bytes accessed | tf_op | source)
XLA Modules:
  0.0 203.7 jit_solution(9323975922391477750)
XLA Ops:
  4.0 19.5 %all_to_all.35 = bf16[4,128,1920]{2,1,0:T(8,128)(2,1)S(1)} all-to-all(bf16[4,128,1920]{2,1,0:T(8,128)(2,1)S(1)} %broadcast_in_dim.10), channel_id=1, replica_groups={{0,64,16,80},{128,192,144,208},{256,320,272,336},{384,448,400,464},{1,6..., dimensions={0} | all-to-all | bytes 3932160 | tf_op jit(solution)/shard_map/all_to_all | solution.py:59
  23.5 2.5 %broadcast_in_dim.12 = bf16[4,512,1152]{2,1,0:T(8,128)(2,1)} broadcast(bf16[512,1152]{1,0:T(8,128)(2,1)S(1)} %bitcast.37), dimensions={1,2} | broadcast | bytes 5898240 | tf_op jit(solution)/shard_map/broadcast_in_dim | solution.py:63
  26.0 5.1 %all-to-all-start.1 = ((bf16[4,512,1152]{2,1,0:T(8,128)(2,1)}), bf16[4,512,1152]{2,1,0:T(8,128)(2,1)}, u32[]{:S(2)}, u32[]{:S(2)}) async-start(bf16[4,512,1152]{2,1,0:T(8,128)(2,1)} %broadcast_in_dim.12), calls=%async_computation.1 | async-start | bytes 9437184 | tf_op jit(solution)/shard_map/all_to_all | solution.py:59
  31.1 7.3 %collective-permute-start = (bf16[128,768]{1,0:T(8,128)(2,1)S(1)}, bf16[128,768]{1,0:T(8,128)(2,1)S(1)}, u32[]{:S(2)}, u32[]{:S(2)}) collective-permute-start(bf16[128,768]{1,0:T(8,128)(2,1)S(1)} %copy-done.1), channel_id=1, source_target_pairs={{0,32},{1,33},{2,34},{3,35},{4,36},{5,37},{6,38},{7,39},{8,40},{9,... | collective-permute-start | bytes 589832 | tf_op jit(solution)/shard_map/ppermute | solution.py:67
  38.4 1.9 collective-permute-start.1
  42.0 2.3 %multiply_reduce_fusion = (f32[256]{0:T(256)S(1)}, f32[256,1152]{1,0:T(8,128)S(1)}) fusion(bf16[1152,768]{1,0:T(8,128)(2,1)} %param.11, bf16[128,768]{1,0:T(8,128)(2,1)S(1)} %collective-permute-done, bf16[128,768]{1,0:T(8,128)(2,1)S(1)} %copy-done.1), kind=kOutput, calls=%fused_computation.31 | convolution fusion | flops 454360832 | bytes 3343360 | tf_op jit(solution)/shard_map/dot_general | solution.py:133
  45.6 15.1 %all-to-all-done.1 = bf16[4,512,1152]{2,1,0:T(8,128)(2,1)} async-done(((bf16[4,512,1152]{2,1,0:T(8,128)(2,1)}), bf16[4,512,1152]{2,1,0:T(8,128)(2,1)}, u32[]{:S(2)}, u32[]{:S(2)}) %all-to-all-start.1) | async-done | bytes 4718624 | tf_op jit(solution)/shard_map/all_to_all | solution.py:59
  60.7 4.3 %fusion.12 = f32[256,2048]{1,0:T(8,128)S(1)} fusion(bf16[2048,1152]{1,0:T(8,128)(2,1)} %bitcast.1, s32[2048]{0:T(1024)S(1)} %bitcast.43, s32[256]{0:T(256)S(1)} %pad_add_fusion, f32[256]{0:T(256)S(1)} %add_rsqrt_fusion, bf16[128,1152]{1,0:T(8,128)(2,1)} %collective-permute-done.1, bf16[128,1152]{1,0:T(8,128)(2,1)S(1)} %copy-done), kind=kOutput, calls=%fused_computation.17 | convolution fusion | flops 1214447616 | bytes 7415808 | tf_op jit(solution)/shard_map/dot_general | solution.py:84
  65.0 4.9 %fusion.15 = (f32[256]{0:T(256)S(1)}, f32[256,2048]{1,0:T(8,128)S(1)}) fusion(f32[256,2048]{1,0:T(8,128)S(1)} %fusion.12, bf16[2048,1152]{1,0:T(8,128)(2,1)} %bitcast.1, f32[256,1152]{1,0:T(8,128)S(1)} %broadcast_multiply_fusion), kind=kOutput, calls=%fused_computation.22 | convolution fusion | flops 1214021376 | bytes 10093568 | tf_op jit(solution)/shard_map/dot_general | solution.py:79
  69.9 3.9 %fusion.18 = f32[256,1152]{1,0:T(8,128)S(1)} fusion(bf16[2048,1152]{1,0:T(8,128)(2,1)} %bitcast.1, f32[256,2048]{1,0:T(8,128)S(1)} %fusion.12, f32[256,2048]{1,0:T(8,128)S(1)} %get-tuple-element.17), kind=kOutput, calls=%fused_computation.32 | convolution fusion | flops 1210580992 | bytes 10092544 | tf_op jit(solution)/shard_map/dot_general | solution.py:91
  73.9 8.3 %collective-permute-start.2 = (f32[128,1152]{1,0:T(8,128)S(1)}, f32[128,1152]{1,0:T(8,128)S(1)}, u32[]{:S(2)}, u32[]{:S(2)}) collective-permute-start(f32[128,1152]{1,0:T(8,128)S(1)} %slice.71), channel_id=1, source_target_pairs={{0,32},{1,33},{2,34},{3,35},{4,36},{5,37},{6,38},{7,39},{8,40},{9,... | collective-permute-start | bytes 1769480 | tf_op jit(solution)/shard_map/ppermute | solution.py:67
  82.2 1.6 collective-permute-done.2
  85.2 8.2 %all_to_all.36 = bf16[4,288,128]{2,1,0:T(8,128)(2,1)S(1)} all-to-all(bf16[4,288,128]{2,1,0:T(8,128)(2,1)S(1)} %bitcast.40), channel_id=1, replica_groups={{0,64,16,80},{128,192,144,208},{256,320,272,336},{384,448,400,464},{1,6..., dimensions={0} | all-to-all | bytes 589824 | tf_op jit(solution)/shard_map/all_to_all | solution.py:59
  94.7 3.5 %all-to-all-start.3 = ((f32[4,72,768]{2,1,0:T(8,128)}), f32[4,72,768]{2,1,0:T(8,128)S(1)}, u32[]{:S(2)}, u32[]{:S(2)}) async-start(f32[4,72,768]{2,1,0:T(8,128)} %bitcast.13), calls=%async_computation.3 | async-start | bytes 1769472 | tf_op jit(solution)/shard_map/all_to_all | solution.py:59
  98.3 8.8 %all-to-all-done.3 = f32[4,72,768]{2,1,0:T(8,128)S(1)} async-done(((f32[4,72,768]{2,1,0:T(8,128)}), f32[4,72,768]{2,1,0:T(8,128)S(1)}, u32[]{:S(2)}, u32[]{:S(2)}) %all-to-all-start.3) | async-done | bytes 884768 | tf_op jit(solution)/shard_map/all_to_all | solution.py:59
  107.2 4.6 %collective-permute-start.3 = (f32[80,384]{1,0:T(8,128)S(1)}, f32[80,384]{1,0:T(8,128)S(1)}, u32[]{:S(2)}, u32[]{:S(2)}) collective-permute-start(f32[80,384]{1,0:T(8,128)S(1)} %select_maximum_fusion), channel_id=1, source_target_pairs={{0,32},{1,33},{2,34},{3,35},{4,36},{5,37},{6,38},{7,39},{8,40},{9,... | collective-permute-start | bytes 368648 | tf_op jit(solution)/shard_map/ppermute | solution.py:67
  113.5 11.2 %all-to-all-start.4 = ((f32[16,9,384]{2,1,0:T(8,128)}), f32[16,9,384]{2,1,0:T(8,128)S(1)}, u32[]{:S(2)}, u32[]{:S(2)}) async-start(f32[16,9,384]{2,1,0:T(8,128)} %pad_maximum_fusion.3), calls=%async_computation.4 | async-start | bytes 786432 | tf_op jit(solution)/shard_map/all_to_all | solution.py:59
  124.8 17.4 %all-to-all-done.4 = f32[16,9,384]{2,1,0:T(8,128)S(1)} async-done(((f32[16,9,384]{2,1,0:T(8,128)}), f32[16,9,384]{2,1,0:T(8,128)S(1)}, u32[]{:S(2)}, u32[]{:S(2)}) %all-to-all-start.4) | async-done | bytes 221216 | tf_op jit(solution)/shard_map/all_to_all | solution.py:59
  143.8 12.5 %all-to-all-start.5 = ((bf16[16,9,384]{2,1,0:T(8,128)(2,1)}), bf16[16,9,384]{2,1,0:T(8,128)(2,1)S(1)}, u32[]{:S(2)}, u32[]{:S(2)}) async-start(bf16[16,9,384]{2,1,0:T(8,128)(2,1)} %broadcast_in_dim.13), calls=%async_computation.5 | async-start | bytes 393216 | tf_op jit(solution)/shard_map/all_to_all | solution.py:59
  156.3 12.5 %all-to-all-done.5 = bf16[16,9,384]{2,1,0:T(8,128)(2,1)S(1)} async-done(((bf16[16,9,384]{2,1,0:T(8,128)(2,1)}), bf16[16,9,384]{2,1,0:T(8,128)(2,1)S(1)}, u32[]{:S(2)}, u32[]{:S(2)}) %all-to-all-start.5) | async-done | bytes 110624 | tf_op jit(solution)/shard_map/all_to_all | solution.py:59
  169.0 17.0 %all_to_all.37 = bf16[16,99,384]{2,1,0:T(8,128)(2,1)S(1)} all-to-all(bf16[16,99,384]{2,1,0:T(8,128)(2,1)S(1)} %broadcast_in_dim.14), channel_id=1, replica_groups={{0,128,256,384,64,192,320,448,16,144,272,400,80,208,336,464},{1,129,257..., dimensions={0} | all-to-all | bytes 2433024 | tf_op jit(solution)/shard_map/all_to_all | solution.py:59
  187.2 8.2 %collective-permute-start.4 = (bf16[16,99,384]{2,0,1:T(8,128)(2,1)}, bf16[16,99,384]{2,0,1:T(8,128)(2,1)S(1)}, u32[]{:S(2)}, u32[]{:S(2)}) collective-permute-start(bf16[16,99,384]{2,0,1:T(8,128)(2,1)} %copy.23), channel_id=1, source_target_pairs={{0,32},{1,33},{2,34},{3,35},{4,36},{5,37},{6,38},{7,39},{8,40},{9,... | collective-permute-start | bytes 3649544 | tf_op jit(solution)/shard_map/ppermute | solution.py:67
  196.0 1.9 collective-permute-done.4
  199.6 4.1 %fusion.2 = bf16[1152,768]{1,0:T(8,128)(2,1)} fusion(bf16[1152,768]{1,0:T(8,128)(2,1)S(1)} %bitcast.38, s32[1152]{0:T(1024)S(1)} %fusion.49), kind=kOutput, calls=%fused_computation.5 | convolution fusion | flops 2040643584 | bytes 3543552 | tf_op jit(solution)/shard_map/dot_general | solution.py:213
  (57 shorter events, 16.1 us)
Async XLA Ops:
  26.0 5.1 %copy-start.1 = (bf16[128,768]{1,0:T(8,128)(2,1)S(1)}, bf16[128,768]{1,0:T(8,128)(2,1)}, u32[]{:S(2)}) copy-start(bf16[128,768]{1,0:T(8,128)(2,1)} %param.7) | copy-start | bytes 589828
  26.0 12.4 %copy-start = (bf16[128,1152]{1,0:T(8,128)(2,1)S(1)}, bf16[128,1152]{1,0:T(8,128)(2,1)}, u32[]{:S(2)}) copy-start(bf16[128,1152]{1,0:T(8,128)(2,1)} %param.8) | copy-start | bytes 884740
  26.0 34.7 %all-to-all-start.1 = ((bf16[4,512,1152]{2,1,0:T(8,128)(2,1)}), bf16[4,512,1152]{2,1,0:T(8,128)(2,1)}, u32[]{:S(2)}, u32[]{:S(2)}) async-start(bf16[4,512,1152]{2,1,0:T(8,128)(2,1)} %broadcast_in_dim.12), calls=%async_computation.1 | async-start | bytes 9437184 | tf_op jit(solution)/shard_map/all_to_all | solution.py:59
  31.1 10.9 %collective-permute-start = (bf16[128,768]{1,0:T(8,128)(2,1)S(1)}, bf16[128,768]{1,0:T(8,128)(2,1)S(1)}, u32[]{:S(2)}, u32[]{:S(2)}) collective-permute-start(bf16[128,768]{1,0:T(8,128)(2,1)S(1)} %copy-done.1), channel_id=1, source_target_pairs={{0,32},{1,33},{2,34},{3,35},{4,36},{5,37},{6,38},{7,39},{8,40},{9,... | collective-permute-start | bytes 589832 | tf_op jit(solution)/shard_map/ppermute | solution.py:67
  38.4 6.0 %collective-permute-start.1 = (bf16[128,1152]{1,0:T(8,128)(2,1)S(1)}, bf16[128,1152]{1,0:T(8,128)(2,1)}, u32[]{:S(2)}, u32[]{:S(2)}) collective-permute-start(bf16[128,1152]{1,0:T(8,128)(2,1)S(1)} %copy-done), channel_id=1, source_target_pairs={{0,32},{1,33},{2,34},{3,35},{4,36},{5,37},{6,38},{7,39},{8,40},{9,... | collective-permute-start | bytes 884744 | tf_op jit(solution)/shard_map/ppermute | solution.py:67
  73.9 9.9 %collective-permute-start.2 = (f32[128,1152]{1,0:T(8,128)S(1)}, f32[128,1152]{1,0:T(8,128)S(1)}, u32[]{:S(2)}, u32[]{:S(2)}) collective-permute-start(f32[128,1152]{1,0:T(8,128)S(1)} %slice.71), channel_id=1, source_target_pairs={{0,32},{1,33},{2,34},{3,35},{4,36},{5,37},{6,38},{7,39},{8,40},{9,... | collective-permute-start | bytes 1769480 | tf_op jit(solution)/shard_map/ppermute | solution.py:67
  94.7 12.3 %all-to-all-start.3 = ((f32[4,72,768]{2,1,0:T(8,128)}), f32[4,72,768]{2,1,0:T(8,128)S(1)}, u32[]{:S(2)}, u32[]{:S(2)}) async-start(f32[4,72,768]{2,1,0:T(8,128)} %bitcast.13), calls=%async_computation.3 | async-start | bytes 1769472 | tf_op jit(solution)/shard_map/all_to_all | solution.py:59
  98.2 44.0 %copy-start.2 = (f32[36,768]{1,0:T(8,128)S(1)}, f32[36,768]{1,0:T(8,128)}, u32[]{:S(2)}) copy-start(f32[36,768]{1,0:T(8,128)} %param.13) | copy-start | bytes 331780
  98.3 44.0 %copy-start.3 = (f32[36,768]{1,0:T(8,128)S(1)}, f32[36,768]{1,0:T(8,128)}, u32[]{:S(2)}) copy-start(f32[36,768]{1,0:T(8,128)} %param.12) | copy-start | bytes 331780
  107.2 5.6 %collective-permute-start.3 = (f32[80,384]{1,0:T(8,128)S(1)}, f32[80,384]{1,0:T(8,128)S(1)}, u32[]{:S(2)}, u32[]{:S(2)}) collective-permute-start(f32[80,384]{1,0:T(8,128)S(1)} %select_maximum_fusion), channel_id=1, source_target_pairs={{0,32},{1,33},{2,34},{3,35},{4,36},{5,37},{6,38},{7,39},{8,40},{9,... | collective-permute-start | bytes 368648 | tf_op jit(solution)/shard_map/ppermute | solution.py:67
  113.5 28.7 %all-to-all-start.4 = ((f32[16,9,384]{2,1,0:T(8,128)}), f32[16,9,384]{2,1,0:T(8,128)S(1)}, u32[]{:S(2)}, u32[]{:S(2)}) async-start(f32[16,9,384]{2,1,0:T(8,128)} %pad_maximum_fusion.3), calls=%async_computation.4 | async-start | bytes 786432 | tf_op jit(solution)/shard_map/all_to_all | solution.py:59
  143.8 25.0 %all-to-all-start.5 = ((bf16[16,9,384]{2,1,0:T(8,128)(2,1)}), bf16[16,9,384]{2,1,0:T(8,128)(2,1)S(1)}, u32[]{:S(2)}, u32[]{:S(2)}) async-start(bf16[16,9,384]{2,1,0:T(8,128)(2,1)} %broadcast_in_dim.13), calls=%async_computation.5 | async-start | bytes 393216 | tf_op jit(solution)/shard_map/all_to_all | solution.py:59
  187.2 10.7 %collective-permute-start.4 = (bf16[16,99,384]{2,0,1:T(8,128)(2,1)}, bf16[16,99,384]{2,0,1:T(8,128)(2,1)S(1)}, u32[]{:S(2)}, u32[]{:S(2)}) collective-permute-start(bf16[16,99,384]{2,0,1:T(8,128)(2,1)} %copy.23), channel_id=1, source_target_pairs={{0,32},{1,33},{2,34},{3,35},{4,36},{5,37},{6,38},{7,39},{8,40},{9,... | collective-permute-start | bytes 3649544 | tf_op jit(solution)/shard_map/ppermute | solution.py:67

commit v2 on v1

--- a/solution.py
+++ b/solution.py
@@ -52,6 +52,7 @@
     for y in range(4)
     for core in range(2)
 ]
+SPLIT = ((0, 3), (3, 4))
 TWIN = [(i, i ^ 32) for i in range(512)]
 
 
@@ -93,15 +94,26 @@
 
 
 def row_order(core):
-    place = lax.iota(jnp.int32, 1152)
-    first, second = place // 288, place // 72 % 4
+    place = lax.iota(jnp.int32, 1280)
+    first, second = place // 320, place // 80 % 4
     X = jnp.where(core == 0, first, second)
     y = jnp.where(core == 0, second, first)
-    return X * 288 + place // 9 % 8 * 36 + y * 9 + place % 9
-
-
-def one_hot(index):
-    return (index[:, None] == lax.iota(jnp.int32, 1152)[None, :]).astype(jnp.bfloat16)
+    row = (X % 2 * 4 + y) * 5 + place % 5
+    return jnp.where(row < 36, X // 2 * 576 + place // 5 % 16 * 36 + row, -1)
+
+
+def place_order(xl):
+    row = lax.iota(jnp.int32, 1152)
+    q = row % 36
+    weights = (row // 576 * 8 + q // 5) * 95 + row // 36 % 16 * 5 + q % 5
+    part = lax.iota(jnp.int32, 120)
+    q = part % 40
+    grads = (xl * 8 + q // 5) * 95 + 80 + part // 40 * 5 + q % 5
+    return jnp.concatenate([weights, grads])
+
+
+def one_hot(index, width):
+    return (index[:, None] == lax.iota(jnp.int32, width)[None, :]).astype(jnp.bfloat16)
 
 
 def rounded(values):
@@ -126,7 +138,12 @@
     texts_b = unit_rows(text_embeds).astype(jnp.bfloat16)
     near = share(jnp.concatenate([texts_b, student_features], axis=1), FIRST)
     features = near[:, :, 1152:]
-    texts = share(near[:, :, :1152].reshape(512, 1152), SECOND).reshape(2048, 1152)
+    texts = []
+    for lo, hi in SPLIT:
+        part = near[lo:hi, :, :1152].reshape((hi - lo) * rows, 1152)
+        if texts:
+            part, texts[-1] = lax.optimization_barrier((part, texts[-1]))
+        texts.append(share(part, SECOND).reshape(-1, 1152))
 
     both_features = jnp.concatenate([student_features, from_twin(student_features)], axis=0)
     both_teacher = jnp.concatenate([teacher_image, from_twin(teacher_image)], axis=0)
@@ -142,7 +159,7 @@
     ids_plane = lax.dynamic_index_in_dim(ids_grid, z, 4, keepdims=False)
     ids_core = lax.dynamic_index_in_dim(ids_plane, core, 2, keepdims=False)
     ids_yx = ids_core.transpose(0, 2, 1, 3).reshape(4, 4, rows)
-    text_ids = jnp.where(core == 0, ids_yx, ids_yx.transpose(1, 0, 2)).reshape(-1)
+    text_ids = jnp.where(core == 0, ids_yx, ids_yx.transpose(1, 0, 2))
     ids_rows = pair_ids.reshape(512, rows)
     left_ids = jnp.concatenate(
         [
@@ -150,7 +167,11 @@
             lax.dynamic_index_in_dim(ids_rows, (blk_index ^ 1) * 32 + group_index, 0, keepdims=False),
         ]
     )
-    losses, pulled = pair_terms(student_b, teacher_b, left_ids, texts, text_ids)
+    terms = [
+        pair_terms(student_b, teacher_b, left_ids, part, text_ids[:, lo:hi].reshape(-1))
+        for part, (lo, hi) in zip(texts, SPLIT)
+    ]
+    losses, pulled = (sum(term) for term in zip(*terms))
 
     pulled = pulled[:rows] + from_twin(pulled[rows:])
     student, inverse = student[:rows], inverse[:rows]
@@ -160,24 +181,24 @@
     ).astype(jnp.bfloat16)
 
     grad_rows = lax.dot_general(
-        one_hot(row_order(core)),
+        one_hot(row_order(core), 1152),
         grad_projected,
         (((1,), (1,)), ((), ())),
         preferred_element_type=jnp.float32,
     ).astype(jnp.bfloat16)
-    grad_rows = exchange(grad_rows.reshape(4, 288, rows), FIRST)
+    grad_rows = exchange(grad_rows.reshape(4, 320, rows), FIRST)
     line_grad = lax.dot_general(
         grad_rows, features, (((0, 2), (0, 1)), ((), ())), preferred_element_type=jnp.float32
     )
-    core_grad = jnp.sum(exchange(line_grad.reshape(4, 72, 768), SECOND), axis=0)
+    core_grad = jnp.sum(exchange(line_grad.reshape(4, 80, 768), SECOND), axis=0)
     left, right = core_grad[:, :384], core_grad[:, 384:]
     other_losses = jnp.pad(losses[rows:].reshape(1, rows), ((0, 7), (0, 256)))
     arrived = from_twin(jnp.concatenate([jnp.where(core == 0, right, left), other_losses], axis=0))
-    chip_grad = jnp.where(core == 0, left, right) + arrived[:72]
-    row_loss = (losses[:rows] + arrived[72, :rows]) / rows
-
-    plane_grad = chip_grad.reshape(8, 9, 384)
-    own_grad = jnp.sum(exchange(jnp.concatenate([plane_grad, plane_grad], axis=0), COLUMN), axis=0)
+    chip_grad = jnp.where(core == 0, left, right) + arrived[:80]
+    row_loss = (losses[:rows] + arrived[80, :rows]) / rows
+
+    column_grad = jnp.pad(chip_grad.reshape(16, 15, 128), ((0, 0), (0, 1), (0, 0)))
+    own_grad = jnp.sum(exchange(column_grad, COLUMN), axis=0)[:15].reshape(5, 384)
 
     def adam(head_grad, first, second, weights):
         new_first = beta_one * first + (1.0 - beta_one) * head_grad
@@ -188,37 +209,38 @@
         updated = weights - learn_rate * (
             first_hat / (jnp.sqrt(second_hat) + adam_eps) + weight_decay * weights
         )
-        return new_first, new_second, updated.astype(jnp.bfloat16)
+        return updated.astype(jnp.bfloat16)
 
     def piece(values, start):
-        return lax.dynamic_slice(values, (start + y * 9, core * 384), (9, 384))
-
-    _, _, own_weights = adam(
+        group_rows = lax.dynamic_slice_in_dim(values, start, 36, 0)
+        padded = jnp.pad(group_rows, ((0, 4), (0, 0)))
+        return lax.dynamic_slice(padded, ((xh * 4 + y) * 5, core * 384), (5, 384))
+
+    own_weights = adam(
         own_grad,
         piece(moment_first, 0),
         piece(moment_second, 0),
         piece(head_weights, group_index * 36),
     )
-    column = share(own_weights, COLUMN)
-    chip_weights = lax.dynamic_slice_in_dim(column, xh * 8, 8, 0).reshape(72, 384)
+    chip_weights = share(own_weights, COLUMN).reshape(80, 384)
     high = rounded(own_grad)
     middle = rounded(own_grad - high)
     low = own_grad - high - middle
     grad_parts = jnp.concatenate([high, middle, low], axis=0).astype(jnp.bfloat16)
-    half = share(jnp.concatenate([chip_weights, grad_parts], axis=0), PLANE)
+    plane = share(jnp.concatenate([chip_weights, grad_parts], axis=0), PLANE)
+    half = lax.dot_general(
+        one_hot(place_order(xl), 1520),
+        plane.reshape(1520, 384),
+        (((1,), (0,)), ((), ())),
+        preferred_element_type=jnp.float32,
+    ).astype(jnp.bfloat16)
     twin_half = from_twin(half)
     whole = jnp.concatenate(
-        [jnp.where(core == 0, half, twin_half), jnp.where(core == 0, twin_half, half)], axis=2
-    )
-    new_weights = lax.dot_general(
-        one_hot(row_order(0)),
-        whole[:, :72].reshape(1152, 768),
-        (((0,), (0,)), ((), ())),
-        preferred_element_type=jnp.float32,
-    ).astype(jnp.bfloat16)
-    parts = lax.dynamic_slice_in_dim(whole, (xl * 2 + z // 8) * 4, 4, 0)[:, 72:]
-    parts = parts.reshape(4, 3, 9, 768).astype(jnp.float32)
-    head_grad = ((parts[:, 0] + parts[:, 1]) + parts[:, 2]).reshape(36, 768)
+        [jnp.where(core == 0, half, twin_half), jnp.where(core == 0, twin_half, half)], axis=1
+    )
+    new_weights = whole[:1152]
+    parts = whole[1152:].reshape(3, 40, 768).astype(jnp.float32)
+    head_grad = ((parts[0] + parts[1]) + parts[2])[:36]
     new_first = beta_one * moment_first + (1.0 - beta_one) * head_grad
     new_second = beta_two * moment_second + (1.0 - beta_two) * head_grad * head_grad
     return (row_loss, new_first, new_second, new_weights)

time: 207 us -> 196 us (0.947)
  waiting for transfers between devices: 58.2 us -> 47.6 us
  starting transfers between devices: 62.5 us -> 55.2 us
  local copies, waits for them, and re-layouts: 6.72 us -> 10.8 us
  blocking collectives: 44.7 us -> 47.8 us
    all_to_all x4 -> x5, waiting for transfers between devices: 53.8 us -> 43.4 us  [exchange(): lax.all_to_all(pieces, AXES, 0, 0, axis_index_groups=groups, tiled=True)]
    all_to_all x4 -> x5, starting transfers between devices: 32.2 us -> 27 us  [exchange(): lax.all_to_all(pieces, AXES, 0, 0, axis_index_groups=groups, tiled=True)]
    all_to_all x3, blocking collectives: 44.7 us -> 47.8 us  [exchange(): lax.all_to_all(pieces, AXES, 0, 0, axis_index_groups=groups, tiled=True)]
    reshape x2 -> x5, local copies, waits for them, and re-layouts: 0.05 us -> 2.24 us  [the longest x1 1.19 us: per_device(): plane.reshape(1520, 384)]
    broadcast_in_dim x4 -> x5, local copies, waits for them, and re-layouts: 3.46 us -> 4.43 us  [share(): jnp.broadcast_to(block[None], (len(groups[0]), *block.shape))]
    dot_general x1 -> x2, matrix products: 3.94 us -> 4.87 us  [pair_terms(): pulled = jnp.dot(coeff, text_rows, preferred_element_type=jnp.float32)]
    dot_general x1 -> x2, matrix products: 4.26 us -> 4.96 us  [pair_terms(): lax.dot_general(teacher_rows, text_rows, dims, preferred_element_type=jnp...]
    dot_general x1 -> x2, matrix products: 4.91 us -> 4.83 us  [pair_terms(): lax.dot_general(student_rows, text_rows, dims, preferred_element_type=jnp...]
  transfers between devices with their start and end apart: 9 -> 10, of which waited for: 7 -> 7; matrix products, arithmetic and copies ran while one was open for 3% -> 9% of each run, Pallas kernels for 0% -> 0%
where the time goes in v2:
time: 196 us; the launch traced here: 194 us
  starting transfers between devices  55.2 us (28%)
  blocking collectives  47.8 us (24%)
  waiting for transfers between devices  47.6 us (24%)
  matrix products  22.7 us (12%)
  local copies, waits for them, and re-layouts  10.8 us (6%)
  other arithmetic  9.17 us (5%)
    all_to_all x3, blocking collectives, exchange(): lax.all_to_all(pieces, AXES, 0, 0, axis_index_groups=groups, tiled=True)  47.8 us
    all_to_all x5, waiting for transfers between devices, exchange(): lax.all_to_all(pieces, AXES, 0, 0, axis_index_groups=groups, tiled=True)  43.4 us
    ppermute x5, starting transfers between devices, from_twin(): return lax.ppermute(shard, AXES, TWIN)  28.2 us
    all_to_all x5, starting transfers between devices, exchange(): lax.all_to_all(pieces, AXES, 0, 0, axis_index_groups=groups, tiled=True)  27 us
    dot_general x2, matrix products, pair_terms(): lax.dot_general(teacher_rows, text_rows, dims, preferred_element_type=jnp...  4.96 us
    dot_general x2, matrix products, pair_terms(): pulled = jnp.dot(coeff, text_rows, preferred_element_type=jnp.float32)  4.87 us
    dot_general x2, matrix products, pair_terms(): lax.dot_general(student_rows, text_rows, dims, preferred_element_type=jnp...  4.83 us
    broadcast_in_dim x5, local copies, waits for them, and re-layouts, share(): jnp.broadcast_to(block[None], (len(groups[0]), *block.shape))  4.43 us
  transfers between devices with their start and end apart: 10, of which 7 were waited for; matrix products, arithmetic and copies ran while one was open for 9% of the time, Pallas kernels for 0%

profile of v2, /device:TPU:1, one launch (start us, length us, event | category | flops | bytes accessed | tf_op | source)
XLA Modules:
  0.0 194.5 jit_solution(4079403793218969355)
XLA Ops:
  4.1 19.5 %all_to_all.40 = bf16[4,128,1920]{2,1,0:T(8,128)(2,1)S(1)} all-to-all(bf16[4,128,1920]{2,1,0:T(8,128)(2,1)S(1)} %broadcast_in_dim.13), channel_id=1, replica_groups={{0,64,16,80},{128,192,144,208},{256,320,272,336},{384,448,400,464},{1,6..., dimensions={0} | all-to-all | bytes 3932160 | tf_op jit(solution)/shard_map/all_to_all | solution.py:60
  25.0 2.0 %broadcast_in_dim.15 = bf16[4,384,1152]{2,1,0:T(8,128)(2,1)} broadcast(bf16[384,1152]{1,0:T(8,128)(2,1)S(1)} %bitcast.45), dimensions={1,2} | broadcast | bytes 4423680 | tf_op jit(solution)/shard_map/broadcast_in_dim | solution.py:64
  27.0 4.9 %all-to-all-start.1 = ((bf16[4,384,1152]{2,1,0:T(8,128)(2,1)}), bf16[4,384,1152]{2,1,0:T(8,128)(2,1)}, u32[]{:S(2)}, u32[]{:S(2)}) async-start(bf16[4,384,1152]{2,1,0:T(8,128)(2,1)} %broadcast_in_dim.15), calls=%async_computation.1 | async-start | bytes 7077888 | tf_op jit(solution)/shard_map/all_to_all | solution.py:60
  31.9 7.3 %collective-permute-start = (bf16[128,768]{1,0:T(8,128)(2,1)S(1)}, bf16[128,768]{1,0:T(8,128)(2,1)S(1)}, u32[]{:S(2)}, u32[]{:S(2)}) collective-permute-start(bf16[128,768]{1,0:T(8,128)(2,1)S(1)} %copy-done.8), channel_id=1, source_target_pairs={{0,32},{1,33},{2,34},{3,35},{4,36},{5,37},{6,38},{7,39},{8,40},{9,... | collective-permute-start | bytes 589832 | tf_op jit(solution)/shard_map/ppermute | solution.py:68
  39.2 1.9 collective-permute-start.1
  47.1 8.0 %all-to-all-done.1 = bf16[4,384,1152]{2,1,0:T(8,128)(2,1)} async-done(((bf16[4,384,1152]{2,1,0:T(8,128)(2,1)}), bf16[4,384,1152]{2,1,0:T(8,128)(2,1)}, u32[]{:S(2)}, u32[]{:S(2)}) %all-to-all-start.1) | async-done | bytes 3538976 | tf_op jit(solution)/shard_map/all_to_all | solution.py:60
  56.3 3.5 %all-to-all-start.2 = ((bf16[4,128,1152]{2,1,0:T(8,128)(2,1)}), bf16[4,128,1152]{2,1,0:T(8,128)(2,1)S(1)}, u32[]{:S(2)}, u32[]{:S(2)}) async-start(bf16[4,128,1152]{2,1,0:T(8,128)(2,1)} %broadcast_in_dim.16), calls=%async_computation.2 | async-start | bytes 2359296 | tf_op jit(solution)/shard_map/all_to_all | solution.py:60
  59.8 3.5 %fusion.12 = f32[256,1536]{1,0:T(8,128)S(1)} fusion(bf16[1536,1152]{1,0:T(8,128)(2,1)} %bitcast.2, s32[1536]{0:T(1024)S(1)} %eq.83, s32[256]{0:T(256)} %pad_add_fusion.1, f32[256]{0:T(256)} %add_rsqrt_fusion, bf16[128,1152]{1,0:T(8,128)(2,1)S(1)} %collective-permute-done.1, bf16[128,1152]{1,0:T(8,128)(2,1)S(1)} %copy-done.7), kind=kOutput, calls=%fused_computation.18 | convolution fusion | flops 911278080 | bytes 5709824 | tf_op jit(solution)/shard_map/dot_general | solution.py:85
  63.4 3.9 %fusion.15 = (f32[256]{0:T(256)S(1)}, f32[256,1536]{1,0:T(8,128)S(1)}) fusion(f32[256,1536]{1,0:T(8,128)S(1)} %fusion.12, bf16[1536,1152]{1,0:T(8,128)(2,1)} %bitcast.2, f32[256,1152]{1,0:T(8,128)S(1)} %copy-done.2), kind=kOutput, calls=%fused_computation.22 | convolution fusion | flops 910589696 | bytes 7865344 | tf_op jit(solution)/shard_map/dot_general | solution.py:80
  67.3 4.3 %fusion.26 = f32[256,1152]{1,0:T(8,128)} fusion(bf16[1536,1152]{1,0:T(8,128)(2,1)} %bitcast.2, f32[256,1536]{1,0:T(8,128)S(1)} %fusion.12, f32[256,1536]{1,0:T(8,128)S(1)} %get-tuple-element.24), kind=kOutput, calls=%fused_computation.42 | convolution fusion | flops 907935744 | bytes 7864320 | tf_op jit(solution)/shard_map/dot_general | solution.py:92
  74.9 8.3 %collective-permute-start.2 = (f32[128,1152]{1,0:T(8,128)S(1)}, f32[128,1152]{1,0:T(8,128)S(1)}, u32[]{:S(2)}, u32[]{:S(2)}) collective-permute-start(f32[128,1152]{1,0:T(8,128)S(1)} %slice.97), channel_id=1, source_target_pairs={{0,32},{1,33},{2,34},{3,35},{4,36},{5,37},{6,38},{7,39},{8,40},{9,... | collective-permute-start | bytes 1769480 | tf_op jit(solution)/shard_map/ppermute | solution.py:68
  86.3 10.2 %all_to_all.41 = bf16[4,320,128]{2,1,0:T(8,128)(2,1)S(1)} all-to-all(bf16[4,320,128]{2,1,0:T(8,128)(2,1)S(1)} %bitcast.46), channel_id=1, replica_groups={{0,64,16,80},{128,192,144,208},{256,320,272,336},{384,448,400,464},{1,6..., dimensions={0} | all-to-all | bytes 655360 | tf_op jit(solution)/shard_map/all_to_all | solution.py:60
  96.4 2.5 %fusion.27 = f32[320,768,1]{1,0,2:T(8,128)} fusion(bf16[4,320,128]{2,1,0:T(8,128)(2,1)S(1)} %all_to_all.41, bf16[4,128,1920]{2,1,0:T(8,128)(2,1)} %copy-done.1), kind=kOutput, calls=%fused_computation.43 | convolution fusion | flops 251658240 | bytes 2097152 | tf_op jit(solution)/shard_map/dot_general | solution.py:190
  98.9 3.5 %all-to-all-start.4 = ((f32[4,80,768]{2,1,0:T(8,128)}), f32[4,80,768]{2,1,0:T(8,128)S(1)}, u32[]{:S(2)}, u32[]{:S(2)}) async-start(f32[4,80,768]{2,1,0:T(8,128)} %bitcast.44), calls=%async_computation.4 | async-start | bytes 1966080 | tf_op jit(solution)/shard_map/all_to_all | solution.py:60
  102.5 9.3 %all-to-all-done.4 = f32[4,80,768]{2,1,0:T(8,128)S(1)} async-done(((f32[4,80,768]{2,1,0:T(8,128)}), f32[4,80,768]{2,1,0:T(8,128)S(1)}, u32[]{:S(2)}, u32[]{:S(2)}) %all-to-all-start.4) | async-done | bytes 983072 | tf_op jit(solution)/shard_map/all_to_all | solution.py:60
  111.9 3.9 %collective-permute-start.3 = (f32[88,384]{1,0:T(8,128)S(1)}, f32[88,384]{1,0:T(8,128)S(1)}, u32[]{:S(2)}, u32[]{:S(2)}) collective-permute-start(f32[88,384]{1,0:T(8,128)S(1)} %select_maximum_fusion), channel_id=1, source_target_pairs={{0,32},{1,33},{2,34},{3,35},{4,36},{5,37},{6,38},{7,39},{8,40},{9,... | collective-permute-start | bytes 405512 | tf_op jit(solution)/shard_map/ppermute | solution.py:68
  117.5 11.2 %all-to-all-start.5 = ((f32[16,16,128]{2,1,0:T(8,128)}), f32[16,16,128]{2,1,0:T(8,128)S(1)}, u32[]{:S(2)}, u32[]{:S(2)}) async-start(f32[16,16,128]{2,1,0:T(8,128)} %pad.22), calls=%async_computation.5 | async-start | bytes 262144 | tf_op jit(solution)/shard_map/all_to_all | solution.py:60
  128.9 12.0 %all-to-all-done.5 = f32[16,16,128]{2,1,0:T(8,128)S(1)} async-done(((f32[16,16,128]{2,1,0:T(8,128)}), f32[16,16,128]{2,1,0:T(8,128)S(1)}, u32[]{:S(2)}, u32[]{:S(2)}) %all-to-all-start.5) | async-done | bytes 131104 | tf_op jit(solution)/shard_map/all_to_all | solution.py:60
  141.1 18.2 %all_to_all.42 = bf16[16,5,384]{2,1,0:T(8,128)(2,1)S(1)} all-to-all(bf16[16,5,384]{2,1,0:T(8,128)(2,1)S(1)} %broadcast_in_dim.17), channel_id=1, replica_groups={{0,1,2,3,4,5,6,7,8,9,10,11,12,13,14,15},{32,33,34,35,36,37,38,39,40,41,..., dimensions={0} | all-to-all | bytes 122880 | tf_op jit(solution)/shard_map/all_to_all | solution.py:60
  160.4 3.9 %all-to-all-start.7 = ((bf16[16,95,384]{2,1,0:T(8,128)(2,1)}), bf16[16,95,384]{2,1,0:T(8,128)(2,1)S(1)}, u32[]{:S(2)}, u32[]{:S(2)}) async-start(bf16[16,95,384]{2,1,0:T(8,128)(2,1)} %broadcast_in_dim.19), calls=%async_computation.7 | async-start | bytes 2359296 | tf_op jit(solution)/shard_map/all_to_all | solution.py:60
  164.4 14.1 %all-to-all-done.7 = bf16[16,95,384]{2,1,0:T(8,128)(2,1)S(1)} async-done(((bf16[16,95,384]{2,1,0:T(8,128)(2,1)}), bf16[16,95,384]{2,1,0:T(8,128)(2,1)S(1)}, u32[]{:S(2)}, u32[]{:S(2)}) %all-to-all-start.7) | async-done | bytes 1167392 | tf_op jit(solution)/shard_map/all_to_all | solution.py:60
  179.6 3.5 %fusion.4 = bf16[1272,384]{1,0:T(8,128)(2,1)S(1)} fusion(bf16[1520,384]{1,0:T(8,128)(2,1)} %reshape.202, s32[1272]{0:T(1024)S(1)} %pad_add_fusion), kind=kOutput, calls=%fused_computation.8 | convolution fusion | flops 1487303808 | bytes 2149344 | tf_op jit(solution)/shard_map/dot_general | solution.py:231
  183.1 6.8 %collective-permute-start.4 = (bf16[1272,384]{1,0:T(8,128)(2,1)S(1)}, bf16[1272,384]{1,0:T(8,128)(2,1)S(1)}, u32[]{:S(2)}, u32[]{:S(2)}) collective-permute-start(bf16[1272,384]{1,0:T(8,128)(2,1)S(1)} %fusion.4), channel_id=1, source_target_pairs={{0,32},{1,33},{2,34},{3,35},{4,36},{5,37},{6,38},{7,39},{8,40},{9,... | collective-permute-start | bytes 2930696 | tf_op jit(solution)/shard_map/ppermute | solution.py:68
  190.5 1.6 collective-permute-done.4
  (82 shorter events, 25.4 us)
Async XLA Ops:
  0.6 42.8 %copy-start = (bf16[1152,768]{1,0:T(8,128)(2,1)S(1)}, bf16[1152,768]{1,0:T(8,128)(2,1)}, u32[]{:S(2)}) copy-start(bf16[1152,768]{1,0:T(8,128)(2,1)} %param.11) | copy-start | bytes 5308420
  23.6 1.4 copy-start.1
  27.0 4.9 %copy-start.8 = (bf16[128,768]{1,0:T(8,128)(2,1)S(1)}, bf16[128,768]{1,0:T(8,128)(2,1)}, u32[]{:S(2)}) copy-start(bf16[128,768]{1,0:T(8,128)(2,1)} %param.7) | copy-start | bytes 589828
  27.0 12.1 %copy-start.7 = (bf16[128,1152]{1,0:T(8,128)(2,1)S(1)}, bf16[128,1152]{1,0:T(8,128)(2,1)}, u32[]{:S(2)}) copy-start(bf16[128,1152]{1,0:T(8,128)(2,1)} %param.8) | copy-start | bytes 884740
  27.0 28.1 %all-to-all-start.1 = ((bf16[4,384,1152]{2,1,0:T(8,128)(2,1)}), bf16[4,384,1152]{2,1,0:T(8,128)(2,1)}, u32[]{:S(2)}, u32[]{:S(2)}) async-start(bf16[4,384,1152]{2,1,0:T(8,128)(2,1)} %broadcast_in_dim.15), calls=%async_computation.1 | async-start | bytes 7077888 | tf_op jit(solution)/shard_map/all_to_all | solution.py:60
  31.9 11.5 %collective-permute-start = (bf16[128,768]{1,0:T(8,128)(2,1)S(1)}, bf16[128,768]{1,0:T(8,128)(2,1)S(1)}, u32[]{:S(2)}, u32[]{:S(2)}) collective-permute-start(bf16[128,768]{1,0:T(8,128)(2,1)S(1)} %copy-done.8), channel_id=1, source_target_pairs={{0,32},{1,33},{2,34},{3,35},{4,36},{5,37},{6,38},{7,39},{8,40},{9,... | collective-permute-start | bytes 589832 | tf_op jit(solution)/shard_map/ppermute | solution.py:68
  39.2 6.2 %collective-permute-start.1 = (bf16[128,1152]{1,0:T(8,128)(2,1)S(1)}, bf16[128,1152]{1,0:T(8,128)(2,1)S(1)}, u32[]{:S(2)}, u32[]{:S(2)}) collective-permute-start(bf16[128,1152]{1,0:T(8,128)(2,1)S(1)} %copy-done.7), channel_id=1, source_target_pairs={{0,32},{1,33},{2,34},{3,35},{4,36},{5,37},{6,38},{7,39},{8,40},{9,... | collective-permute-start | bytes 884744 | tf_op jit(solution)/shard_map/ppermute | solution.py:68
  44.2 39.1 %copy-start.9 = (f32[256]{0:T(256)}, f32[256]{0:T(256)S(1)}, u32[]{:S(2)}) copy-start(f32[256]{0:T(256)S(1)} %add_rsqrt_fusion.1) | copy-start | bytes 3076
  56.3 15.4 %all-to-all-start.2 = ((bf16[4,128,1152]{2,1,0:T(8,128)(2,1)}), bf16[4,128,1152]{2,1,0:T(8,128)(2,1)S(1)}, u32[]{:S(2)}, u32[]{:S(2)}) async-start(bf16[4,128,1152]{2,1,0:T(8,128)(2,1)} %broadcast_in_dim.16), calls=%async_computation.2 | async-start | bytes 2359296 | tf_op jit(solution)/shard_map/all_to_all | solution.py:60
  59.8 3.6 %copy-start.2 = (f32[256,1152]{1,0:T(8,128)S(1)}, f32[256,1152]{1,0:T(8,128)}, u32[]{:S(2)}) copy-start(f32[256,1152]{1,0:T(8,128)} %broadcast_multiply_fusion) | copy-start | bytes 3538948
  67.3 4.3 %copy-start.10 = (s32[256]{0:T(256)S(1)}, s32[256]{0:T(256)}, u32[]{:S(2)}) copy-start(s32[256]{0:T(256)} %pad_add_fusion.1) | copy-start | bytes 3076
  71.6 1.4 copy-start.3
  73.1 1.3 copy-start.4
  74.9 9.9 %collective-permute-start.2 = (f32[128,1152]{1,0:T(8,128)S(1)}, f32[128,1152]{1,0:T(8,128)S(1)}, u32[]{:S(2)}, u32[]{:S(2)}) collective-permute-start(f32[128,1152]{1,0:T(8,128)S(1)} %slice.97), channel_id=1, source_target_pairs={{0,32},{1,33},{2,34},{3,35},{4,36},{5,37},{6,38},{7,39},{8,40},{9,... | collective-permute-start | bytes 1769480 | tf_op jit(solution)/shard_map/ppermute | solution.py:68
  83.3 1.7 slice-start
  98.9 12.9 %all-to-all-start.4 = ((f32[4,80,768]{2,1,0:T(8,128)}), f32[4,80,768]{2,1,0:T(8,128)S(1)}, u32[]{:S(2)}, u32[]{:S(2)}) async-start(f32[4,80,768]{2,1,0:T(8,128)} %bitcast.44), calls=%async_computation.4 | async-start | bytes 1966080 | tf_op jit(solution)/shard_map/all_to_all | solution.py:60
  102.5 38.4 %copy-start.5 = (f32[36,768]{1,0:T(8,128)S(1)}, f32[36,768]{1,0:T(8,128)}, u32[]{:S(2)}) copy-start(f32[36,768]{1,0:T(8,128)} %param.13) | copy-start | bytes 331780
  102.5 38.4 %copy-start.6 = (f32[36,768]{1,0:T(8,128)S(1)}, f32[36,768]{1,0:T(8,128)}, u32[]{:S(2)}) copy-start(f32[36,768]{1,0:T(8,128)} %param.12) | copy-start | bytes 331780
  111.9 4.9 %collective-permute-start.3 = (f32[88,384]{1,0:T(8,128)S(1)}, f32[88,384]{1,0:T(8,128)S(1)}, u32[]{:S(2)}, u32[]{:S(2)}) collective-permute-start(f32[88,384]{1,0:T(8,128)S(1)} %select_maximum_fusion), channel_id=1, source_target_pairs={{0,32},{1,33},{2,34},{3,35},{4,36},{5,37},{6,38},{7,39},{8,40},{9,... | collective-permute-start | bytes 405512 | tf_op jit(solution)/shard_map/ppermute | solution.py:68
  117.5 23.3 %all-to-all-start.5 = ((f32[16,16,128]{2,1,0:T(8,128)}), f32[16,16,128]{2,1,0:T(8,128)S(1)}, u32[]{:S(2)}, u32[]{:S(2)}) async-start(f32[16,16,128]{2,1,0:T(8,128)} %pad.22), calls=%async_computation.5 | async-start | bytes 262144 | tf_op jit(solution)/shard_map/all_to_all | solution.py:60
  160.4 18.0 %all-to-all-start.7 = ((bf16[16,95,384]{2,1,0:T(8,128)(2,1)}), bf16[16,95,384]{2,1,0:T(8,128)(2,1)S(1)}, u32[]{:S(2)}, u32[]{:S(2)}) async-start(bf16[16,95,384]{2,1,0:T(8,128)(2,1)} %broadcast_in_dim.19), calls=%async_computation.7 | async-start | bytes 2359296 | tf_op jit(solution)/shard_map/all_to_all | solution.py:60
  183.1 9.0 %collective-permute-start.4 = (bf16[1272,384]{1,0:T(8,128)(2,1)S(1)}, bf16[1272,384]{1,0:T(8,128)(2,1)S(1)}, u32[]{:S(2)}, u32[]{:S(2)}) collective-permute-start(bf16[1272,384]{1,0:T(8,128)(2,1)S(1)} %fusion.4), channel_id=1, source_target_pairs={{0,32},{1,33},{2,34},{3,35},{4,36},{5,37},{6,38},{7,39},{8,40},{9,... | collective-permute-start | bytes 2930696 | tf_op jit(solution)/shard_map/ppermute | solution.py:68
